TPU v7x, 256 devices: a whole 4x4x8 slice. The times are simulated.
256 devices in a mesh: pairs: 64 (over z, x, core), win: 4 (over y).
Axes of the slice: x: 4, y: 4, z: 8, core: 2. Of those that a mesh axis runs over, the one named last changes fastest.
Arguments:
- raw_traces: bfloat16 [4, 320, 128, 512], P('win', None, 'pairs'), may hold values from -6 to 6
- tile_pairs: int32 [64, 4, 2], replicated, may hold values from -1 to 319, as said below
- block_slot: int32 [320], replicated, may hold values from 0 to 319, as said below
- win_offset: int32 [4], P('win'), may hold values from 0 to 128
Outputs:
- stacks: float32 [128, 256, 128, 128], P('win', 'pairs')
Inputs may be any that keep to these rules, and one draw needn't show every extreme that they name: `tile_pairs`: row p lists owner p's tiles: pairs of block numbers, then rows of -1. Each owner has 1 to 4 tiles and some owner exactly 4. The blocks named in one owner's row are all different. `block_slot`: each slot holds exactly one block.
All inputs are finite; a program needn't handle non-finite values.
Results may differ from a plain program's by a relative error of at most 0.0041.
Values may be sent and summed in bfloat16 or wider, within the bound.
A program may use at most 192 MiB of HBM per device.

v0:
```python
import math

import jax
import jax.numpy as jnp
from jax import lax
from jax.sharding import PartitionSpec as P

LAGS = 128


eps = 1e-06


def whiten(signal):
    length = signal.shape[-1]
    width = LAGS
    radius = LAGS // 2
    seg_count = length // width
    magnitude = jnp.abs(signal).reshape(signal.shape[:-1] + (seg_count, width))
    padded = jnp.pad(magnitude, [(0, 0)] * (magnitude.ndim - 2) + [(1, 1), (0, 0)])
    windows = jnp.concatenate([padded[..., :-2, :], padded[..., 1:-1, :], padded[..., 2:, :]], -1)
    rowpos = jnp.arange(3 * width)[:, None]
    colpos = jnp.arange(width)[None, :]
    band_matrix = (jnp.abs(rowpos - width - colpos) <= radius).astype(jnp.float32)
    totals = jnp.einsum(
        "...ni,ij->...nj", windows, band_matrix, precision=lax.Precision.HIGHEST
    ).reshape(signal.shape)
    position = jnp.arange(length)
    tally = (jnp.minimum(position, radius) + jnp.minimum(length - 1 - position, radius) + 1).astype(
        jnp.float32
    )
    return (signal / (totals / tally + eps)).astype(jnp.bfloat16)


def correlate(leading_blocks, trailing_blocks):
    seg_len = leading_blocks.shape[-1]
    samples = seg_len - LAGS
    half = LAGS // 2
    kernel = jnp.transpose(leading_blocks[..., half : half + samples], (1, 0, 2))
    source = jnp.transpose(trailing_blocks[..., : seg_len - 1], (1, 0, 2))
    return lax.conv_general_dilated(
        source,
        kernel,
        (1,),
        "VALID",
        dimension_numbers=("NCH", "OIH", "CNH"),
        preferred_element_type=jnp.float32,
    )


def body(raw_traces, tile_pairs, block_slot, win_offset):
    owner_index = lax.axis_index("pairs")
    pair_count = lax.axis_size("pairs")
    win_count = lax.axis_size("win")
    local_channels = raw_traces.shape[2]
    channels = local_channels * pair_count
    seg_len = raw_traces.shape[3] - LAGS
    samples = seg_len - LAGS
    tile_count = tile_pairs.shape[1]
    segment = lax.dynamic_slice_in_dim(raw_traces[0], win_offset[0], seg_len, 2).astype(jnp.float32)
    whitened = whiten(segment)
    wanted = tile_pairs.reshape(pair_count, 2 * tile_count)
    slot_index = block_slot[jnp.maximum(wanted, 0)]
    outgoing = jnp.take(whitened, slot_index.reshape(-1), axis=0).reshape(
        pair_count, 2 * tile_count, local_channels, seg_len
    )
    incoming = lax.all_to_all(outgoing, "pairs", split_axis=0, concat_axis=2, tiled=True)
    blocks = incoming[0].reshape(tile_count, 2, channels, seg_len)
    own_tiles = lax.dynamic_index_in_dim(tile_pairs, owner_index, 0, keepdims=False)
    tile_valid = (own_tiles[:, 0] >= 0).astype(jnp.float32)
    firsts = blocks[:, 0]
    seconds = blocks[:, 1]
    row_share = channels // win_count
    spread_rows = lax.all_to_all(firsts[:, None], "win", split_axis=2, concat_axis=1, tiled=True)
    initial = jnp.zeros((row_share, tile_count, channels, LAGS), jnp.float32)
    piece = lax.all_gather(seconds[:, None], "win", axis=1, tiled=True)
    summed = initial + jnp.stack(
        [correlate(spread_rows[tile], piece[tile]) for tile in range(tile_count)], 1
    )
    scale = 1.0 / math.sqrt(win_count * samples)
    return summed * scale * tile_valid[None, :, None, None]


def solution(mesh):
    return jax.shard_map(
        body,
        mesh=mesh,
        in_specs=(P("win", None, "pairs", None), P(), P(), P("win")),
        out_specs=P("win", "pairs", None, None),
        check_vma=False,
    )
```

profile of v0, /device:TPU:1, one launch (start us, length us, event | category | flops | bytes accessed | tf_op | source)
XLA Modules:
  0.0 132.8 jit_solution(15492690190346590132)
XLA Ops:
  6.5 0.0 copy-start
  6.5 0.0 copy-start.1
  6.5 0.0 all-gather.2.cloned.1.call-start
  7.3 0.7 broadcast_maximum_fusion
  8.0 0.1 copy.86
  8.1 0.2 reshape.108
  8.3 0.0 copy-done.1
  8.3 3.5 %gather_fusion = s32[512]{0:T(512)S(1)} fusion(s32[320]{0:T(512)S(1)} %copy-done.1, s32[1024]{0:T(1024)S(1)} %pad_clamp_fusion.1), kind=kCustom, calls=%fused_computation | custom fusion | bytes 6144 | tf_op jit(solution)/shard_map/gather | solution.py:63
  11.8 0.1 reshape.107
  11.9 0.0 copy-done
  11.9 0.9 constant_dynamic-slice_fusion.1
  12.8 0.1 convert_abs_fusion
  12.9 0.4 copy.88
  13.3 0.4 copy.89
  13.7 0.1 pad_slice_fusion.1
  13.8 1.8 %fusion = f32[320,2,3,128]{0,3,2,1:T(8,128)S(1)} fusion(f32[320,2,3,128]{3,0,2,1:T(8,128)S(1)} %get-tuple-element.10, f32[320,2,3,128]{3,0,2,1:T(8,128)S(1)} %copy.89, f32[320,2,3,128]{3,0,2,1:T(8,128)S(1)} %get-tuple-element.9, s32[384]{0:T(512)S(1)} %iota_add_fusion), kind=kOutput, calls=%fused_computation.3 | convolution fusion | flops 1134084096 | bytes 3933696 | tf_op jit(solution)/shard_map/...ni,ij->...nj/dot_general | solution.py:25
  15.7 0.3 copy.92
  16.0 0.2 fusion.7
  16.2 0.5 copy.93
  16.7 3.1 %gather_fusion.1 = bf16[512,2,384]{2,1,0:T(2,128)(2,1)S(1)} fusion(bf16[320,2,384]{2,1,0:T(2,128)(2,1)S(1)} %copy.93, s32[1024]{0:T(1024)S(1)} %pad_clamp_fusion), kind=kCustom, calls=%fused_computation.1 | custom fusion | bytes 1574912 | tf_op jit(solution)/shard_map/jit(_take)/gather | solution.py:64
  19.8 0.2 bitcast_select_fusion
  20.0 0.1 copy.95
  20.1 35.5 %all_to_all.24 = bf16[64,8,2,384]{3,1,2,0:T(8,128)(2,1)S(1)} all-to-all(bf16[64,8,2,384]{3,1,2,0:T(8,128)(2,1)S(1)} %copy.95), channel_id=1, replica_groups=mesh['pairs'=64,'win'=4] {'pairs'}, dimensions={0} | all-to-all | bytes 1572864 | tf_op jit(solution)/shard_map/all_to_all | solution.py:67
  55.7 0.3 reshape.126
  56.0 1.1 fusion.24
  57.1 0.0 copy-start.2
  57.1 0.8 copy.136
  57.9 0.0 all-gather.2.cloned.1.call-update
  57.9 0.9 copy.99
  58.9 4.2 %all-to-all-start.1 = ((bf16[4,1,128,384]{3,0,1,2:T(4,128)(2,1)}), bf16[4,1,128,384]{3,0,1,2:T(4,128)(2,1)S(1)}, u32[]{:S(2)}, u32[]{:S(2)}) async-start(bf16[4,1,128,384]{3,0,1,2:T(4,128)(2,1)} %copy.99), calls=%async_computation.1 | async-start | bytes 786432 | tf_op jit(solution)/shard_map/all_to_all | solution.py:74
  63.0 0.0 copy-done.2
  63.0 0.1 constant_dynamic-slice_fusion
  63.1 0.1 copy.111
  63.2 6.4 %all-to-all-done.1 = bf16[4,1,128,384]{3,0,1,2:T(4,128)(2,1)S(1)} async-done(((bf16[4,1,128,384]{3,0,1,2:T(4,128)(2,1)}), bf16[4,1,128,384]{3,0,1,2:T(4,128)(2,1)S(1)}, u32[]{:S(2)}, u32[]{:S(2)}) %all-to-all-start.1) | async-done | bytes 393248 | tf_op jit(solution)/shard_map/all_to_all | solution.py:74
  69.6 0.6 fusion.25
  70.2 0.1 slice.86
  70.3 0.1 slice.92
  70.4 0.1 slice.89
  70.5 0.1 slice.95
  70.6 0.2 copy.130
  70.8 0.2 copy.124
  71.0 0.2 copy.127
  71.2 0.9 copy.121
  72.1 12.6 %all-gather.2.cloned.1.call-done = bf16[4,4,128,384]{3,2,0,1:T(8,128)(2,1)} async-done(((bf16[4,1,128,384]{3,2,0,1:T(8,128)(2,1)}), bf16[4,4,128,384]{3,2,0,1:T(8,128)(2,1)}) %all-gather.2.cloned.1.call-update) | async-done | bytes 1572880 | tf_op jit(solution)/shard_map/all_gather | solution.py:76
  84.6 1.5 %fusion.23 = (bf16[1,4,128,384]{3,2,0,1:T(8,128)(2,1)S(1)}, bf16[1,4,128,384]{3,2,0,1:T(8,128)(2,1)S(1)}, bf16[1,4,128,384]{3,2,0,1:T(8,128)(2,1)S(1)}, bf16[1,4,128,384]{3,2,0,1:T(8,128)(2,1)S(1)}) fusion(bf16[4,4,128,384]{3,2,0,1:T(8,128)(2,1)} %all-gather.2.cloned.1.call-done), kind=kLoop, calls=%fused_computation.48 | loop fusion | bytes 3145728 | tf_op jit(solution)/shard_map/slice | solution.py:78
  86.2 0.2 copy.118
  86.4 0.2 copy.125
  86.7 0.2 copy.122
  87.0 0.2 copy.128
  87.2 6.9 %convolution_bitcast_fusion.3 = f32[32,1,128,128]{2,0,3,1:T(8,128)S(1)} fusion(bf16[4,32,256]{1,0,2:T(4,128)(2,1)} %copy.121, bf16[1,4,128,384]{2,1,3,0:T(4,128)(2,1)S(1)} %copy.118), kind=kOutput, calls=%fused_computation.14 | convolution fusion | flops 1073741824 | bytes 2555904 | tf_op jit(solution)/shard_map/conv_general_dilated | solution.py:41
  94.1 5.9 %convolution_bitcast_fusion.1 = f32[32,1,128,128]{2,0,3,1:T(8,128)S(1)} fusion(bf16[4,32,256]{1,0,2:T(4,128)(2,1)S(1)} %copy.127, bf16[1,4,128,384]{2,1,3,0:T(4,128)(2,1)S(1)} %copy.125), kind=kOutput, calls=%fused_computation.12 | convolution fusion | flops 1073741824 | bytes 2555904 | tf_op jit(solution)/shard_map/conv_general_dilated | solution.py:41
  99.9 6.1 %convolution_bitcast_fusion.2 = f32[32,1,128,128]{2,0,3,1:T(8,128)S(1)} fusion(bf16[4,32,256]{1,0,2:T(4,128)(2,1)S(1)} %copy.124, bf16[1,4,128,384]{2,1,3,0:T(4,128)(2,1)S(1)} %copy.122), kind=kOutput, calls=%fused_computation.13 | convolution fusion | flops 1073741824 | bytes 2555904 | tf_op jit(solution)/shard_map/conv_general_dilated | solution.py:41
  106.0 5.9 %convolution_bitcast_fusion = f32[32,1,128,128]{2,0,3,1:T(8,128)S(1)} fusion(bf16[4,32,256]{1,0,2:T(4,128)(2,1)S(1)} %copy.130, bf16[1,4,128,384]{2,1,3,0:T(4,128)(2,1)S(1)} %copy.128), kind=kOutput, calls=%fused_computation.11 | convolution fusion | flops 1073741824 | bytes 2555904 | tf_op jit(solution)/shard_map/conv_general_dilated | solution.py:41
  111.9 4.1 %maximum_multiply_fusion = f32[32,4,128,128]{2,0,3,1:T(8,128)} fusion(f32[32,1,128,128]{2,0,3,1:T(8,128)S(1)} %convolution_bitcast_fusion, f32[32,1,128,128]{2,0,3,1:T(8,128)S(1)} %convolution_bitcast_fusion.1, f32[32,1,128,128]{2,0,3,1:T(8,128)S(1)} %convolution_bitcast_fusion.2, f32[32,1,128,128]{2,0,3,1:T(8,128)S(1)} %convolution_bitcast_fusion.3, ...), kind=kLoop, calls=%fused_computation.2 | loop fusion | flops 8388608 | bytes 16777232 | tf_op jit(solution)/shard_map/mul | solution.py:81
  116.0 9.9 %copy.112 = f32[32,4,128,128]{3,2,1,0:T(8,128)} copy(f32[32,4,128,128]{2,0,3,1:T(8,128)} %maximum_multiply_fusion) | data formatting | bytes 16777216 | tf_op jit(solution)/shard_map/mul | solution.py:81
  (11 shorter events, 0.1 us)
Async XLA Ops:
  6.5 5.4 %copy-start = (bf16[1,320,2,512]{3,2,1,0:T(2,128)(2,1)S(1)}, bf16[1,320,2,512]{3,2,1,0:T(2,128)(2,1)}, u32[]{:S(2)}) copy-start(bf16[1,320,2,512]{3,2,1,0:T(2,128)(2,1)} %param.4) | copy-start | bytes 1966084
  6.5 1.7 %copy-start.1 = (s32[320]{0:T(512)S(1)}, s32[320]{0:T(512)}, u32[]{:S(2)}) copy-start(s32[320]{0:T(512)} %param.6) | copy-start | bytes 3844
  6.5 78.1 %all-gather.2.cloned.1.call-start = ((), (), s32[]{:S(2)}) async-start(), calls=%async_computation.2 | async-start | bytes 1966080 | tf_op jit(solution)/shard_map/all_gather | solution.py:76
  57.1 6.0 %copy-start.2 = (s32[64,4,2]{0,2,1:T(2,128)S(1)}, s32[64,4,2]{0,2,1:T(2,128)}, u32[]{:S(2)}) copy-start(s32[64,4,2]{0,2,1:T(2,128)} %param.5) | copy-start | bytes 6148
  58.9 10.7 %all-to-all-start.1 = ((bf16[4,1,128,384]{3,0,1,2:T(4,128)(2,1)}), bf16[4,1,128,384]{3,0,1,2:T(4,128)(2,1)S(1)}, u32[]{:S(2)}, u32[]{:S(2)}) async-start(bf16[4,1,128,384]{3,0,1,2:T(4,128)(2,1)} %copy.99), calls=%async_computation.1 | async-start | bytes 786432 | tf_op jit(solution)/shard_map/all_to_all | solution.py:74
Sparse Core Ops, SparseCore 0:
  58.0 26.5 all-gather.1
where the time goes:
time: 133 us
  blocking collectives  35.5 us (27%)
  local copies, waits for them, and re-layouts  27.8 us (21%)
  matrix products  26.5 us (20%)
  waiting for transfers between devices  19 us (14%)
  between operations  14.4 us (11%)
  other arithmetic  5.36 us (4%)
  starting transfers between devices  4.18 us (3%)
    all_to_all x1, blocking collectives, body(): lax.all_to_all(outgoing, 'pairs', split_axis=0, concat_axis=2, tiled=True)  35.5 us
    conv_general_dilated x4, matrix products, correlate(): lax.conv_general_dilated(source, kernel, (1,), 'VALID', dimension_numbers...  24.7 us
    all_gather x1, waiting for transfers between devices, body(): piece = lax.all_gather(seconds[:, None], 'win', axis=1, tiled=True)  12.6 us
    mul x1, local copies, waits for them, and re-layouts, body(): return summed * scale * tile_valid[None, :, None, None]  9.9 us
    all_to_all x1, waiting for transfers between devices, body(): lax.all_to_all(firsts[:, None], 'win', split_axis=2, concat_axis=1, tiled...  6.37 us
    all_to_all x1, starting transfers between devices, body(): lax.all_to_all(firsts[:, None], 'win', split_axis=2, concat_axis=1, tiled...  4.18 us
    mul x2, other arithmetic, body(): return summed * scale * tile_valid[None, :, None, None]  4.14 us
    gather x2, local copies, waits for them, and re-layouts, body(): slot_index = block_slot[jnp.maximum(wanted, 0)]  3.57 us
  transfers between devices with their start and end apart: 2, of which 2 were waited for; matrix products, arithmetic and copies ran while one was open for 3% of the time, Pallas kernels for 0%

commit v1 on v0

v1 whole, which is shorter than its diff:
```python
import math

import jax
import jax.numpy as jnp
from jax import lax
from jax.experimental import pallas as pl
from jax.experimental.pallas import tpu as pltpu
from jax.sharding import PartitionSpec as P

LAGS = 128
RADIUS = 64
SEG = 384
SAMPLES = 256
TILES = 4
NP = 64
NW = 4
ROWS = 32
SUB = 16
FULL = 60
BF = jnp.bfloat16
F32 = jnp.float32
MESH = pl.DeviceIdType.MESH
VMEM = pl.BlockSpec(memory_space=pltpu.VMEM)
SMEM = pl.BlockSpec(memory_space=pltpu.SMEM)
DMA = pltpu.SemaphoreType.DMA


def nt(a, b):
    return lax.dot_general(a, b, (((1,), (1,)), ((), ())), preferred_element_type=F32)


def prepare(raw, pairs, slots, offset, seconds, firsts):
    off = offset[0]
    rec = raw.shape[1]
    lanes = raw.shape[0]
    row = lax.broadcasted_iota(jnp.int32, (rec, SEG), 0) - off
    col = lax.broadcasted_iota(jnp.int32, (rec, SEG), 1)
    pick = (row == col).astype(BF)
    band = ((jnp.abs(row - col) <= RADIUS) & (row >= 0) & (row < SEG)).astype(BF)
    x = raw[...]
    segment = jnp.dot(x, pick, preferred_element_type=F32)
    totals = jnp.dot(jnp.abs(x), band, preferred_element_type=F32)
    at = lax.broadcasted_iota(jnp.int32, (1, SEG), 1)
    tally = (jnp.minimum(at, RADIUS) + jnp.minimum(SEG - 1 - at, RADIUS) + 1).astype(F32)
    white = (segment / (totals / tally + 1e-6)).astype(BF)

    slot = slots[...]
    parts = jnp.concatenate([slot // SUB, slot % SUB], 0).astype(F32).astype(BF)
    nblk = slot.shape[1]
    wanted = pairs[...]
    blk = lax.broadcasted_iota(jnp.int32, (2 * NP, nblk), 1)
    lane = lax.broadcasted_iota(jnp.int32, (2 * NP, lanes), 1)
    chan = lax.broadcasted_iota(jnp.int32, (2 * NP, 1), 0) % 2
    for k in range(TILES):
        for j in range(2):
            want = wanted[:, 2 * k + j : 2 * k + j + 1]
            found = nt((want == blk).astype(BF), parts)
            where = (SUB * found[:, 0:1] + found[:, 1:2]).astype(jnp.int32)
            source = jnp.where(want >= 0, 2 * where + chan, -1)
            rows = jnp.dot((source == lane).astype(BF), white, preferred_element_type=F32)
            if j:
                seconds[k] = rows.astype(BF)
            else:
                firsts[k] = rows[:, RADIUS : RADIUS + SAMPLES].astype(BF)


def prepare_kernel(raw, pairs, slots, offset, seconds, firsts):
    prepare(raw, pairs, slots, offset, seconds, firsts)


def exchange_kernel(out_s, out_f, got_s, got_f, send_s, recv_s, send_f, recv_f, send_y, recv_y, recv_y2):
    p = lax.axis_index("pairs")
    y = lax.axis_index("win")
    right, left, far = lax.rem(y + 1, NW), lax.rem(y + 3, NW), lax.rem(y + 2, NW)
    keeper = p // SUB
    barrier = pltpu.get_barrier_semaphore()

    def signal(q, w):
        pl.semaphore_signal(barrier, inc=1, device_id=(q, w), device_id_type=MESH)

    def greet(i, _):
        signal(lax.rem(p + i, NP), y)
        return 0

    lax.fori_loop(1, NP, greet, 0)
    signal(p, right)
    signal(p, left)

    def greet_first(i, _):
        q, w = SUB * y + lax.rem(i, SUB), i // SUB

        @pl.when(jnp.logical_not((q == p) & (w == y)))
        def _():
            signal(q, w)

        return 0

    lax.fori_loop(0, NP, greet_first, 0)
    pl.semaphore_wait(barrier, jnp.where(keeper == y, 2 * NP, 2 * NP + 1))

    mine = pl.ds(pl.multiple_of(2 * p, 2), 2)

    def pair_rows(q):
        return pl.ds(pl.multiple_of(2 * q, 2), 2)

    def wait(ref, sem):
        pltpu.make_async_copy(ref, ref, sem).wait()

    def send_tile(k):
        pltpu.make_async_copy(out_s.at[k, mine], got_s.at[y, k, mine], recv_s.at[k]).start()

        def one(i, _):
            q = lax.rem(p + lax.rem(i * 27, NP), NP)
            pltpu.make_async_remote_copy(
                src_ref=out_s.at[k, pair_rows(q)],
                dst_ref=got_s.at[y, k, mine],
                send_sem=send_s.at[jnp.maximum(i - FULL, 0)],
                recv_sem=recv_s.at[k],
                device_id=(q, y),
                device_id_type=MESH,
            ).start()
            return 0

        lax.fori_loop(1, NP, one, 0)

    kept = pl.ds(pl.multiple_of(2 * lax.rem(p, SUB), 2), 2)

    def send_first(q, sem):
        pltpu.make_async_remote_copy(
            src_ref=out_f.at[:, pair_rows(q)],
            dst_ref=got_f.at[y, :, kept],
            send_sem=send_f.at[sem],
            recv_sem=recv_f,
            device_id=(q, keeper),
            device_id_type=MESH,
        ).start()

    def send_firsts():
        def one(i, _):
            send_first(lax.rem(p + lax.rem(i * 27, NP), NP), jnp.maximum(i - FULL, 0))
            return 0

        lax.fori_loop(1, NP, one, 0)

        @pl.when(keeper == y)
        def _():
            pltpu.make_async_copy(out_f.at[:, mine], got_f.at[y, :, kept], recv_f).start()

        @pl.when(keeper != y)
        def _():
            send_first(p, NP - FULL)

    send_tile(0)
    send_firsts()
    for k in range(1, TILES):
        send_tile(k)

    half = got_s.shape[2] // 2

    def part(w, k, which=None):
        if which is None:
            return got_s.at[w, k]
        return got_s.at[w, k, pl.ds(which * half, half)]

    def pass_on(ref, send, recv, w):
        pltpu.make_async_remote_copy(
            src_ref=ref, dst_ref=ref, send_sem=send, recv_sem=recv, device_id=(p, w), device_id_type=MESH
        ).start()

    def first_step(k):
        wait(part(y, k), recv_s.at[k])
        pass_on(part(y, k), send_y.at[k, 0], recv_y.at[k, 0], right)
        pass_on(part(y, k), send_y.at[k, 1], recv_y.at[k, 1], left)

    def second_step(k):
        wait(part(left, k), recv_y.at[k, 0])
        pass_on(part(left, k, 0), send_y.at[k, 2], recv_y2.at[k, 0], right)
        wait(part(right, k), recv_y.at[k, 1])
        pass_on(part(right, k, 1), send_y.at[k, 3], recv_y2.at[k, 1], left)

    first_step(0)
    for k in range(1, TILES):
        first_step(k)
        second_step(k - 1)
    second_step(TILES - 1)
    for k in range(TILES):
        wait(part(far, k, 0), recv_y2.at[k, 0])
        wait(part(far, k, 1), recv_y2.at[k, 1])
    wait(got_f, recv_f)

    for out, sem in ((out_s, send_s), (out_f, send_f)):
        wait(out.at[:, pl.ds(0, 2 * FULL)], sem.at[0])
        for i in range(1, NP - FULL):
            wait(out.at[:, mine], sem.at[i])

    @pl.when(keeper != y)
    def _():
        wait(out_f.at[:, mine], send_f.at[NP - FULL])

    for k in range(TILES):
        wait(part(y, k), send_y.at[k, 0])
        wait(part(y, k), send_y.at[k, 1])
        wait(part(left, k, 0), send_y.at[k, 2])
        wait(part(right, k, 1), send_y.at[k, 3])


def correlate(second, first, wide, tall, flat):
    zeros = jnp.zeros((ROWS, LAGS), BF)
    for w in range(NW):
        tall[w] = second[w, 0].T
    for s in range(SUB):
        tails = []
        for w in range(NW):
            padded = jnp.concatenate([first[w, 0], zeros], 1)
            moved = pltpu.roll(padded, s, 1) if s else padded
            wide[pl.ds(s * ROWS, ROWS), pl.ds(w * SAMPLES, SAMPLES)] = moved[:, :SAMPLES]
            tail = moved[:, SAMPLES:]
            tails.append(pltpu.roll(tail, SUB * w, 1) if w else tail)
        wide[pl.ds(s * ROWS, ROWS), pl.ds(NW * SAMPLES, LAGS)] = tails[0] + tails[1] + tails[2] + tails[3]
    depth = NW * SAMPLES + NW * SUB
    for pair in range(LAGS // SUB // 2):
        sides = []
        for m in (2 * pair, 2 * pair + 1):
            pieces = [tall[w, pl.ds(SUB * m, SAMPLES)] for w in range(NW)]
            pieces += [tall[w, pl.ds(SUB * m + SAMPLES, SUB)] for w in range(NW)]
            sides.append(jnp.concatenate(pieces, 0))
        right = jnp.concatenate(sides, 1)
        both = jnp.dot(wide[:, :depth], right, preferred_element_type=F32)
        flat[2 * pair] = both[:, :LAGS]
        flat[2 * pair + 1] = both[:, LAGS:]


def correlate_kernel(second, first, out, wide, tall, flat):
    correlate(second, first, wide, tall, flat)
    scale = 1.0 / math.sqrt(NW * SAMPLES)

    def one(c, _):
        rows = [flat[m, pl.ds(c, SUB, stride=ROWS)] for m in range(LAGS // SUB)]
        out[c, 0] = (jnp.concatenate(rows, 0) * scale).T
        return 0

    lax.fori_loop(0, ROWS, one, 0, unroll=4)


def body(raw_traces, tile_pairs, block_slot, win_offset):
    nblk, local, rec = raw_traces.shape[1:]
    raw = raw_traces.reshape(nblk * local, rec)
    pairs = jnp.repeat(tile_pairs.reshape(NP, 2 * TILES), local, axis=0)
    seconds, firsts = pl.pallas_call(
        prepare_kernel,
        out_shape=[
            jax.ShapeDtypeStruct((TILES, 2 * NP, SEG), BF),
            jax.ShapeDtypeStruct((TILES, 2 * NP, SAMPLES), BF),
        ],
        in_specs=[VMEM, VMEM, VMEM, SMEM],
        out_specs=[VMEM, VMEM],
        name="prepare",
    )(raw, pairs, block_slot.reshape(1, nblk), win_offset)
    got_s, got_f = pl.pallas_call(
        exchange_kernel,
        out_shape=[
            jax.ShapeDtypeStruct((NW, TILES, 2 * NP, SEG), BF),
            jax.ShapeDtypeStruct((NW, TILES, ROWS, SAMPLES), BF),
        ],
        in_specs=[VMEM, VMEM],
        out_specs=[VMEM, VMEM],
        scratch_shapes=[
            DMA((NP - FULL,)),
            DMA((TILES,)),
            DMA((NP - FULL + 1,)),
            DMA,
            DMA((TILES, 4)),
            DMA((TILES, 2)),
            DMA((TILES, 2)),
        ],
        compiler_params=pltpu.CompilerParams(collective_id=0, has_side_effects=True),
        name="exchange",
    )(seconds, firsts)
    return pl.pallas_call(
        correlate_kernel,
        grid=(TILES,),
        out_shape=jax.ShapeDtypeStruct((ROWS, TILES, 2 * NP, LAGS), F32),
        in_specs=[
            pl.BlockSpec((NW, 1, 2 * NP, SEG), lambda k: (0, k, 0, 0)),
            pl.BlockSpec((NW, 1, ROWS, SAMPLES), lambda k: (0, k, 0, 0)),
        ],
        out_specs=pl.BlockSpec((ROWS, 1, 2 * NP, LAGS), lambda k: (0, k, 0, 0)),
        scratch_shapes=[
            pltpu.VMEM((SUB * ROWS, NW * SAMPLES + LAGS), BF),
            pltpu.VMEM((NW, SEG, 2 * NP), BF),
            pltpu.VMEM((LAGS // SUB, SUB * ROWS, LAGS), F32),
        ],
        compiler_params=pltpu.CompilerParams(vmem_limit_bytes=32 << 20),
        name="correlate",
    )(got_s, got_f)


def solution(mesh):
    return jax.shard_map(
        body,
        mesh=mesh,
        in_specs=(P("win", None, "pairs", None), P(), P(), P("win")),
        out_specs=P("win", "pairs", None, None),
        check_vma=False,
    )
```

time: 133 us -> 74.4 us (0.56)
  Pallas kernels: 0 us -> 65.5 us
  blocking collectives: 35.5 us -> 0 us
  matrix products: 26.5 us -> 0 us
  local copies, waits for them, and re-layouts: 27.8 us -> 7.74 us
  waiting for transfers between devices: 19 us -> 0 us
  between operations: 14.4 us -> 0.67 us
  other arithmetic: 5.36 us -> 0 us
  starting transfers between devices: 4.18 us -> 0 us
    pallas_call x0 -> x3, Pallas kernels: none -> 65.5 us  [the longest x1 43.6 us: body(): pl.pallas_call(exchange_kernel, out_shape=[jax.ShapeDtypeStruct((NW, TILE...]
    all_to_all x1 -> x0, blocking collectives: 35.5 us -> none  [body(): lax.all_to_all(outgoing, 'pairs', split_axis=0, concat_axis=2, tiled=True)]
    conv_general_dilated x4 -> x0, matrix products: 24.7 us -> none  [correlate(): lax.conv_general_dilated(source, kernel, (1,), 'VALID', dimension_numbers...]
    all_gather x1 -> x0, waiting for transfers between devices: 12.6 us -> none  [body(): piece = lax.all_gather(seconds[:, None], 'win', axis=1, tiled=True)]
    mul x1 -> x0, local copies, waits for them, and re-layouts: 9.9 us -> none  [body(): return summed * scale * tile_valid[None, :, None, None]]
    gather x3 -> x0, local copies, waits for them, and re-layouts: 6.65 us -> none  [the longest x2 3.57 us: body(): slot_index = block_slot[jnp.maximum(wanted, 0)]]
    all_to_all x1 -> x0, waiting for transfers between devices: 6.37 us -> none  [body(): lax.all_to_all(firsts[:, None], 'win', split_axis=2, concat_axis=1, tiled...]
    slice x9 -> x0, local copies, waits for them, and re-layouts: 4.63 us -> none  [the longest x1 1.54 us: body(): piece[tile]]
  transfers between devices with their start and end apart: 2 -> 0, of which waited for: 2 -> 0; matrix products, arithmetic and copies ran while one was open for 3% -> 0% of each run, Pallas kernels for 0% -> 0%
where the time goes in v1:
time: 74.4 us; the launch traced here: 73.9 us
  Pallas kernels  65.5 us (88%)
  local copies, waits for them, and re-layouts  7.74 us (10%)
    pallas_call x1, Pallas kernels, body(): pl.pallas_call(exchange_kernel, out_shape=[jax.ShapeDtypeStruct((NW, TILE...  43.6 us
    pallas_call x1, Pallas kernels, body(): pl.pallas_call(correlate_kernel, grid=(TILES,), out_shape=jax.ShapeDtypeS...  15.5 us
    pallas_call x1, Pallas kernels, body(): pl.pallas_call(prepare_kernel, out_shape=[jax.ShapeDtypeStruct((TILES, 2...  6.35 us
    reshape x1, local copies, waits for them, and re-layouts, body(): raw = raw_traces.reshape(nblk * local, rec)  2.71 us
    unnamed x4, local copies, waits for them, and re-layouts  2.35 us

profile of v1, /device:TPU:1, one launch (start us, length us, event | category | flops | bytes accessed | tf_op | source)
XLA Modules:
  0.0 73.9 jit_solution(11571112233172442399)
XLA Ops:
  0.7 1.3 %reshape.15.slots = s32[1,320]{1,0:T(1,128)} reshape(s32[320]{0:T(512)} %param.6) | data formatting | bytes 2560 | tf_op jit(solution)/shard_map/reshape | solution.py:258
  1.9 0.8 %copy.5 = s32[64,8]{1,0:T(8,128)S(1)} copy(s32[64,8]{0,1:T(8,128)} %bitcast.3) | data formatting | bytes 4096 | tf_op jit(solution)/shard_map/reshape | solution.py:248
  2.7 0.6 broadcast_in_dim.3
  3.3 2.7 %reshape.12.raw = bf16[640,512]{1,0:T(8,128)(2,1)} reshape(bf16[1,320,2,512]{3,2,1,0:T(2,128)(2,1)} %param.4) | data formatting | bytes 1310720 | tf_op jit(solution)/shard_map/reshape | solution.py:247
  6.0 6.4 %prepare.1 = (bf16[4,128,384]{2,1,0:T(8,128)(2,1)}, bf16[4,128,256]{2,1,0:T(8,128)(2,1)}) custom-call(bf16[640,512]{1,0:T(8,128)(2,1)} %reshape.12.raw, s32[128,8]{1,0:T(8,128)} %bitcast.2, s32[1,320]{1,0:T(1,128)} %reshape.15.slots, s32[1]{0:T(128)S(6)} %copy.6.offset), custom_call_target="tpu_custom_call" | custom-call | tf_op jit(solution)/shard_map/prepare/pallas_call | solution.py:249
  12.4 43.6 %exchange.1 = (bf16[4,4,128,384]{3,2,1,0:T(8,128)(2,1)}, bf16[4,4,32,256]{3,2,1,0:T(8,128)(2,1)}) custom-call(bf16[4,128,384]{2,1,0:T(8,128)(2,1)} %get-tuple-element.9.out_s, bf16[4,128,256]{2,1,0:T(8,128)(2,1)} %get-tuple-element.10.out_f), custom_call_target="tpu_custom_call" | custom-call | tf_op jit(solution)/shard_map/exchange/pallas_call | solution.py:259
  56.0 0.0 copy-start
  56.1 1.4 %copy-done = bf16[4,4,128,384]{3,2,1,0:T(8,128)(2,1)S(1)} copy-done((bf16[4,4,128,384]{3,2,1,0:T(8,128)(2,1)S(1)}, bf16[4,4,128,384]{3,2,1,0:T(8,128)(2,1)}, u32[]{:S(2)}) %copy-start) | copy-done | bytes 1572888
  57.5 0.0 copy-start.1
  57.5 0.9 %copy-done.1 = bf16[4,4,32,256]{3,2,1,0:T(8,128)(2,1)S(1)} copy-done((bf16[4,4,32,256]{3,2,1,0:T(8,128)(2,1)S(1)}, bf16[4,4,32,256]{3,2,1,0:T(8,128)(2,1)}, u32[]{:S(2)}) %copy-start.1) | copy-done | bytes 262168
  58.4 15.5 %correlate.1 = f32[32,4,128,128]{3,2,1,0:T(8,128)} custom-call(bf16[4,4,128,384]{3,2,1,0:T(8,128)(2,1)S(1)} %copy-done, bf16[4,4,32,256]{3,2,1,0:T(8,128)(2,1)S(1)} %copy-done.1), custom_call_target="tpu_custom_call" | custom-call | tf_op jit(solution)/shard_map/correlate/pallas_call | solution.py:279
Async XLA Ops:
  56.0 1.4 %copy-start = (bf16[4,4,128,384]{3,2,1,0:T(8,128)(2,1)S(1)}, bf16[4,4,128,384]{3,2,1,0:T(8,128)(2,1)}, u32[]{:S(2)}) copy-start(bf16[4,4,128,384]{3,2,1,0:T(8,128)(2,1)} %get-tuple-element.11.second) | copy-start | bytes 4718596
  57.5 0.9 %copy-start.1 = (bf16[4,4,32,256]{3,2,1,0:T(8,128)(2,1)S(1)}, bf16[4,4,32,256]{3,2,1,0:T(8,128)(2,1)}, u32[]{:S(2)}) copy-start(bf16[4,4,32,256]{3,2,1,0:T(8,128)(2,1)} %get-tuple-element.12.first) | copy-start | bytes 786436
